TPU v7x, 32 devices: a whole 2x2x4 slice. The times are simulated.
32 devices in a mesh: section: 4 (over y, x), state: 8 (over z, core).
Axes of the slice: x: 2, y: 2, z: 4, core: 2. Of those that a mesh axis runs over, the one named last changes fastest.
Arguments:
- belief: float32 [4, 512, 2048], P('section', None, 'state'), may hold values from 0 to 0.04
- action: int32 [4, 512], P('section'), may hold values from 0 to 7
- next_index: int32 [4, 512, 32], P('section'), may hold values from 0 to 511, as said below
- obs_table: float32 [8, 32, 2048], P(None, None, 'state'), may hold values from -1 to 1
- transition: bfloat16 [8, 2048, 2048], P(None, 'state'), may hold values from -0.1875 to 0.1875
- reward: float32 [8, 2048], P(None, 'state'), may hold values from -6 to 6
- terminal: float32 [512, 2048], P(None, 'state'), may hold values from -6 to 6
Outputs:
- alphas: float32 [4, 512, 2048], P('section', None, 'state')
- values: float32 [4, 512], P('section')
Inputs may be any that keep to these rules, and one draw needn't show every extreme that they name: next_index[h, b, o] < 128 * (b // 128 + 1): a belief of micro-batch m names only next-section alpha vectors of micro-batches 0 to m.
All inputs are finite; a program needn't handle non-finite values.
Results may differ from a plain program's by a relative error of at most 0.012.
Values sent between devices are 32-bit elements; how exact they have to be, the bound alone decides.
No kernel may reach another device: no remote copies, remote signals or barrier semaphores. Data moves between devices by JAX's collectives and lax.ppermute only.
A program may use at most 64 MiB of HBM per device.

v0:
```python
import jax
import jax.numpy as jnp
from jax import lax
from jax.sharding import PartitionSpec as P

discount = 0.95


def backup(next_alphas, act_rows, next_rows, belief_rows, obs_table, transition, reward):
    actions = obs_table.shape[0]
    local_width = obs_table.shape[2]
    row_count = act_rows.shape[0]
    picked = next_alphas[next_rows]
    per_action = jnp.einsum("bos,aos->bas", picked, obs_table, precision=lax.Precision.HIGHEST)
    onehot = (act_rows[:, None] == jnp.arange(actions, dtype=jnp.int32)[None, :]).astype(
        jnp.float32
    )
    masked = (
        (per_action * onehot[:, :, None])
        .astype(jnp.bfloat16)
        .reshape(row_count, actions * local_width)
    )
    trans_flat = transition.reshape(actions * local_width, transition.shape[2])
    partial_value = jnp.dot(masked, trans_flat, preferred_element_type=jnp.float32)
    summed = lax.psum_scatter(partial_value, "state", scatter_dimension=1, tiled=True)
    reward_rows = jnp.dot(onehot, reward, precision=lax.Precision.HIGHEST)
    section_alphas = reward_rows + discount * summed
    section_values = lax.psum(jnp.sum(belief_rows * section_alphas, axis=1), "state")
    return (section_alphas, section_values)


def local(belief, action, next_index, obs_table, transition, reward, terminal):
    section_index = lax.axis_index("section")
    sections = lax.axis_size("section")
    beliefs = terminal.shape[0]
    local_width = terminal.shape[1]
    share = beliefs // sections
    every_action, every_next = (
        lax.all_gather(action, "section", axis=0, tiled=True),
        lax.all_gather(next_index, "section", axis=0, tiled=True),
    )
    shared_belief = lax.all_to_all(belief, "section", split_axis=1, concat_axis=0, tiled=True)
    offset = section_index * share

    def turn(turn_number, carry):
        nextset, kept_alphas, kept_values = carry
        horizon_step = (sections - 1 - turn_number).astype(jnp.int32)
        act_section = lax.dynamic_index_in_dim(every_action, horizon_step, 0, False)
        next_section_rows = lax.dynamic_index_in_dim(every_next, horizon_step, 0, False)
        act_rows = lax.dynamic_slice_in_dim(act_section, offset, share, 0)
        next_rows = lax.dynamic_slice_in_dim(next_section_rows, offset, share, 0)
        belief_rows = lax.dynamic_index_in_dim(shared_belief, horizon_step, 0, False)
        part_alphas, part_values = backup(
            nextset, act_rows, next_rows, belief_rows, obs_table, transition, reward
        )
        nextset = lax.all_gather(part_alphas, "section", axis=0, tiled=True)
        kept_alphas = lax.dynamic_update_index_in_dim(kept_alphas, part_alphas, horizon_step, 0)
        kept_values = lax.dynamic_update_index_in_dim(kept_values, part_values, horizon_step, 0)
        return (nextset, kept_alphas, kept_values)

    start = (
        terminal,
        jnp.zeros((sections, share, local_width), jnp.float32),
        jnp.zeros((sections, share), jnp.float32),
    )
    result = lax.fori_loop(0, sections, turn, start)
    out_alphas, out_values = (
        lax.all_to_all(result[1], "section", split_axis=0, concat_axis=1, tiled=True),
        lax.all_to_all(result[2], "section", split_axis=0, concat_axis=1, tiled=True),
    )
    return (out_alphas, out_values)


def solution(mesh):
    return jax.shard_map(
        local,
        mesh=mesh,
        in_specs=(
            P("section", None, "state"),
            P("section", None),
            P("section", None, None),
            P(None, None, "state"),
            P(None, "state", None),
            P(None, "state"),
            P(None, "state"),
        ),
        out_specs=(P("section", None, "state"), P("section", None)),
        check_vma=False,
    )
```

profile of v0, /device:TPU:0, one launch (start us, length us, event | category | flops | bytes accessed | tf_op | source)
XLA Modules:
  0.0 433.7 jit_solution(1737412535606526940)
XLA Ops:
  14.7 11.2 %all-gather = s32[4,1,512]{2,1,0:T(1,128)S(1)} all-gather(s32[1,1,512]{2,1,0:T(1,128)} %bitcast.64), channel_id=1, replica_groups=mesh['section'=4,'state'=8] {'section'}, dimensions={0}, use_global_device_ids=true | all-gather | bytes 10240 | tf_op jit(solution)/shard_map/all_gather | solution.py:39
  27.4 11.3 %copy.20 = bf16[8,256,2048]{2,0,1:T(8,128)(2,1)} copy(bf16[8,256,2048]{2,1,0:T(8,128)(2,1)} %param.13) | data formatting | bytes 16777216 | tf_op jit(solution)/shard_map/while | solution.py:66
  38.7 8.0 %all_gather.18 = s32[4,512,32]{1,2,0:T(8,128)S(1)} all-gather(s32[1,512,32]{1,2,0:T(8,128)S(1)} %copy-done.2), channel_id=1, replica_groups=mesh['section'=4,'state'=8] {'section'}, dimensions={0}, use_global_device_ids=true | all-gather | bytes 327680 | tf_op jit(solution)/shard_map/all_gather | solution.py:40
  47.6 360.7 %while.20 = (s32[]{:T(128)}, f32[512,256]{1,0:T(8,128)S(1)}, f32[4,128,256]{2,1,0:T(8,128)}, f32[4,128]{1,0:T(4,128)S(1)}, s32[4,512]{1,0:T(4,128)S(1)}, /*index...) while((s32[]{:T(128)}, f32[512,256]{1,0:T(8,128)S(1)}, ...), condition=%wide.region_4.5_spmd, body=%wide.region_0.4_spmd.sunk | while | flops 1178225664 | bytes 36770572 | solution.py:66
  47.9 16.1 %gather_fusion = f32[4096,256]{1,0:T(8,128)} fusion(f32[512,256]{1,0:T(8,128)S(1)} %get-tuple-element.453, s32[4096]{0:T(1024)S(1)} %broadcast_clamp_fusion.2), kind=kCustom, calls=%fused_computation.clone.1 | custom fusion | bytes 8404992 | tf_op jit(solution)/shard_map/while/body/eval_jaxpr/gather | solution.py:13
  64.0 5.9 %copy.29 = f32[128,32,256]{0,1,2:T(8,128)} copy(f32[128,32,256]{2,1,0:T(8,128)} %bitcast.57) | data formatting | bytes 8388608 | tf_op jit(solution)/shard_map/while/body/eval_jaxpr/gather | solution.py:13
  70.0 5.5 %fusion.24 = bf16[128,8,256]{0,1,2:T(8,128)(2,1)S(1)} fusion(f32[128,32,256]{0,1,2:T(8,128)} %copy.29, f32[8,32,256]{1,0,2:T(8,128)S(1)} %get-tuple-element.475, f32[128,8]{0,1:T(8,128)S(1)} %fusion.23), kind=kOutput, calls=%fused_computation.4.clone.1 | convolution fusion | flops 101187584 | bytes 4984832 | tf_op jit(solution)/shard_map/while/body/eval_jaxpr/bos,aos->bas/dot_general | solution.py:14
  75.5 5.8 %convolution_bitcast_fusion.2 = f32[128,2048]{1,0:T(8,128)} fusion(bf16[128,8,256]{0,1,2:T(8,128)(2,1)S(1)} %fusion.24, bf16[8,256,2048]{2,0,1:T(8,128)(2,1)} %get-tuple-element.476), kind=kOutput, calls=%fused_computation.1.clone.1 | convolution fusion | flops 1073741824 | bytes 9961472 | tf_op jit(solution)/shard_map/while/body/eval_jaxpr/dot_general | solution.py:24
  81.3 33.0 %reduce-scatter.2.cloned.1.call-done = f32[128,256]{1,0:T(8,128)} async-done(((f32[128,2048]{1,0:T(8,128)}), f32[128,256]{1,0:T(8,128)}) %reduce-scatter.2.cloned.1.call-update) | async-done | bytes 131088 | tf_op jit(solution)/shard_map/while/body/eval_jaxpr/reduce_scatter | solution.py:25
  116.1 10.1 %all_gather.20 = f32[512,256]{1,0:T(8,128)S(1)} all-gather(f32[128,256]{1,0:T(8,128)S(1)} %get-tuple-element.435), channel_id=1, replica_groups=mesh['section'=4,'state'=8] {'section'}, dimensions={0}, use_global_device_ids=true | all-gather | bytes 655360 | tf_op jit(solution)/shard_map/while/body/eval_jaxpr/all_gather | solution.py:56
  126.3 13.7 %psum.16 = f32[1,128]{1,0:T(1,128)S(1)} all-reduce(f32[1,128]{1,0:T(1,128)S(1)} %bitcast.61), channel_id=1, replica_groups=mesh['section'=4,'state'=8] {'state'}, use_global_device_ids=true, to_apply=%region_3.3 | all-reduce | flops 128 | bytes 1024 | tf_op jit(solution)/shard_map/while/body/eval_jaxpr/psum | solution.py:28
  140.4 16.1 %gather_fusion = f32[4096,256]{1,0:T(8,128)} fusion(f32[512,256]{1,0:T(8,128)S(1)} %get-tuple-element.453, s32[4096]{0:T(1024)S(1)} %broadcast_clamp_fusion.2), kind=kCustom, calls=%fused_computation.clone.1 | custom fusion | bytes 8404992 | tf_op jit(solution)/shard_map/while/body/eval_jaxpr/gather | solution.py:13
  156.5 5.9 %copy.29 = f32[128,32,256]{0,1,2:T(8,128)} copy(f32[128,32,256]{2,1,0:T(8,128)} %bitcast.57) | data formatting | bytes 8388608 | tf_op jit(solution)/shard_map/while/body/eval_jaxpr/gather | solution.py:13
  162.5 5.5 %fusion.24 = bf16[128,8,256]{0,1,2:T(8,128)(2,1)S(1)} fusion(f32[128,32,256]{0,1,2:T(8,128)} %copy.29, f32[8,32,256]{1,0,2:T(8,128)S(1)} %get-tuple-element.475, f32[128,8]{0,1:T(8,128)S(1)} %fusion.23), kind=kOutput, calls=%fused_computation.4.clone.1 | convolution fusion | flops 101187584 | bytes 4984832 | tf_op jit(solution)/shard_map/while/body/eval_jaxpr/bos,aos->bas/dot_general | solution.py:14
  168.0 5.8 %convolution_bitcast_fusion.2 = f32[128,2048]{1,0:T(8,128)} fusion(bf16[128,8,256]{0,1,2:T(8,128)(2,1)S(1)} %fusion.24, bf16[8,256,2048]{2,0,1:T(8,128)(2,1)} %get-tuple-element.476), kind=kOutput, calls=%fused_computation.1.clone.1 | convolution fusion | flops 1073741824 | bytes 9961472 | tf_op jit(solution)/shard_map/while/body/eval_jaxpr/dot_general | solution.py:24
  173.8 30.0 %reduce-scatter.2.cloned.1.call-done = f32[128,256]{1,0:T(8,128)} async-done(((f32[128,2048]{1,0:T(8,128)}), f32[128,256]{1,0:T(8,128)}) %reduce-scatter.2.cloned.1.call-update) | async-done | bytes 131088 | tf_op jit(solution)/shard_map/while/body/eval_jaxpr/reduce_scatter | solution.py:25
  205.6 10.0 %all_gather.20 = f32[512,256]{1,0:T(8,128)S(1)} all-gather(f32[128,256]{1,0:T(8,128)S(1)} %get-tuple-element.435), channel_id=1, replica_groups=mesh['section'=4,'state'=8] {'section'}, dimensions={0}, use_global_device_ids=true | all-gather | bytes 655360 | tf_op jit(solution)/shard_map/while/body/eval_jaxpr/all_gather | solution.py:56
  215.7 13.7 %psum.16 = f32[1,128]{1,0:T(1,128)S(1)} all-reduce(f32[1,128]{1,0:T(1,128)S(1)} %bitcast.61), channel_id=1, replica_groups=mesh['section'=4,'state'=8] {'state'}, use_global_device_ids=true, to_apply=%region_3.3 | all-reduce | flops 128 | bytes 1024 | tf_op jit(solution)/shard_map/while/body/eval_jaxpr/psum | solution.py:28
  229.8 16.1 %gather_fusion = f32[4096,256]{1,0:T(8,128)} fusion(f32[512,256]{1,0:T(8,128)S(1)} %get-tuple-element.453, s32[4096]{0:T(1024)S(1)} %broadcast_clamp_fusion.2), kind=kCustom, calls=%fused_computation.clone.1 | custom fusion | bytes 8404992 | tf_op jit(solution)/shard_map/while/body/eval_jaxpr/gather | solution.py:13
  245.9 5.9 %copy.29 = f32[128,32,256]{0,1,2:T(8,128)} copy(f32[128,32,256]{2,1,0:T(8,128)} %bitcast.57) | data formatting | bytes 8388608 | tf_op jit(solution)/shard_map/while/body/eval_jaxpr/gather | solution.py:13
  257.3 5.8 %convolution_bitcast_fusion.2 = f32[128,2048]{1,0:T(8,128)} fusion(bf16[128,8,256]{0,1,2:T(8,128)(2,1)S(1)} %fusion.24, bf16[8,256,2048]{2,0,1:T(8,128)(2,1)} %get-tuple-element.476), kind=kOutput, calls=%fused_computation.1.clone.1 | convolution fusion | flops 1073741824 | bytes 9961472 | tf_op jit(solution)/shard_map/while/body/eval_jaxpr/dot_general | solution.py:24
  263.1 30.0 %reduce-scatter.2.cloned.1.call-done = f32[128,256]{1,0:T(8,128)} async-done(((f32[128,2048]{1,0:T(8,128)}), f32[128,256]{1,0:T(8,128)}) %reduce-scatter.2.cloned.1.call-update) | async-done | bytes 131088 | tf_op jit(solution)/shard_map/while/body/eval_jaxpr/reduce_scatter | solution.py:25
  295.0 10.0 %all_gather.20 = f32[512,256]{1,0:T(8,128)S(1)} all-gather(f32[128,256]{1,0:T(8,128)S(1)} %get-tuple-element.435), channel_id=1, replica_groups=mesh['section'=4,'state'=8] {'section'}, dimensions={0}, use_global_device_ids=true | all-gather | bytes 655360 | tf_op jit(solution)/shard_map/while/body/eval_jaxpr/all_gather | solution.py:56
  305.1 13.7 %psum.16 = f32[1,128]{1,0:T(1,128)S(1)} all-reduce(f32[1,128]{1,0:T(1,128)S(1)} %bitcast.61), channel_id=1, replica_groups=mesh['section'=4,'state'=8] {'state'}, use_global_device_ids=true, to_apply=%region_3.3 | all-reduce | flops 128 | bytes 1024 | tf_op jit(solution)/shard_map/while/body/eval_jaxpr/psum | solution.py:28
  319.1 16.1 %gather_fusion = f32[4096,256]{1,0:T(8,128)} fusion(f32[512,256]{1,0:T(8,128)S(1)} %get-tuple-element.453, s32[4096]{0:T(1024)S(1)} %broadcast_clamp_fusion.2), kind=kCustom, calls=%fused_computation.clone.1 | custom fusion | bytes 8404992 | tf_op jit(solution)/shard_map/while/body/eval_jaxpr/gather | solution.py:13
  335.2 5.9 %copy.29 = f32[128,32,256]{0,1,2:T(8,128)} copy(f32[128,32,256]{2,1,0:T(8,128)} %bitcast.57) | data formatting | bytes 8388608 | tf_op jit(solution)/shard_map/while/body/eval_jaxpr/gather | solution.py:13
  346.7 5.8 %convolution_bitcast_fusion.2 = f32[128,2048]{1,0:T(8,128)} fusion(bf16[128,8,256]{0,1,2:T(8,128)(2,1)S(1)} %fusion.24, bf16[8,256,2048]{2,0,1:T(8,128)(2,1)} %get-tuple-element.476), kind=kOutput, calls=%fused_computation.1.clone.1 | convolution fusion | flops 1073741824 | bytes 9961472 | tf_op jit(solution)/shard_map/while/body/eval_jaxpr/dot_general | solution.py:24
  352.5 30.1 %reduce-scatter.2.cloned.1.call-done = f32[128,256]{1,0:T(8,128)} async-done(((f32[128,2048]{1,0:T(8,128)}), f32[128,256]{1,0:T(8,128)}) %reduce-scatter.2.cloned.1.call-update) | async-done | bytes 131088 | tf_op jit(solution)/shard_map/while/body/eval_jaxpr/reduce_scatter | solution.py:25
  384.4 10.0 %all_gather.20 = f32[512,256]{1,0:T(8,128)S(1)} all-gather(f32[128,256]{1,0:T(8,128)S(1)} %get-tuple-element.435), channel_id=1, replica_groups=mesh['section'=4,'state'=8] {'section'}, dimensions={0}, use_global_device_ids=true | all-gather | bytes 655360 | tf_op jit(solution)/shard_map/while/body/eval_jaxpr/all_gather | solution.py:56
  394.5 13.7 %psum.16 = f32[1,128]{1,0:T(1,128)S(1)} all-reduce(f32[1,128]{1,0:T(1,128)S(1)} %bitcast.61), channel_id=1, replica_groups=mesh['section'=4,'state'=8] {'state'}, use_global_device_ids=true, to_apply=%region_3.3 | all-reduce | flops 128 | bytes 1024 | tf_op jit(solution)/shard_map/while/body/eval_jaxpr/psum | solution.py:28
  408.2 7.2 %all_to_all.40 = f32[4,1,128]{2,1,0:T(1,128)S(1)} all-to-all(f32[4,1,128]{2,1,0:T(1,128)S(1)} %bitcast.62), channel_id=1, replica_groups=mesh['section'=4,'state'=8] {'section'}, dimensions={0} | all-to-all | bytes 4096 | tf_op jit(solution)/shard_map/all_to_all | solution.py:69
  418.9 6.9 %all-to-all-done.1 = f32[4,128,256]{2,1,0:T(8,128)S(1)} async-done(((f32[4,128,256]{2,1,0:T(8,128)}), f32[4,128,256]{2,1,0:T(8,128)S(1)}, u32[]{:S(2)}, u32[]{:S(2)}) %all-to-all-start.1) | async-done | bytes 524320 | tf_op jit(solution)/shard_map/all_to_all | solution.py:68
  (67 shorter events, 35.1 us)
Async XLA Ops:
  9.5 37.1 %all-to-all-start = ((f32[1,512,256]{2,0,1:T(1,128)}), f32[1,512,256]{2,0,1:T(1,128)S(1)}, u32[]{:S(2)}, u32[]{:S(2)}) async-start(f32[1,512,256]{2,0,1:T(1,128)} %copy.17), calls=%async_computation.1 | async-start | bytes 1048576 | tf_op jit(solution)/shard_map/all_to_all | solution.py:42
  27.3 11.3 %copy-start.2 = (s32[1,512,32]{1,2,0:T(8,128)S(1)}, s32[1,512,32]{1,2,0:T(8,128)}, u32[]{:S(2)}) copy-start(s32[1,512,32]{1,2,0:T(8,128)} %param.11) | copy-start | bytes 196612
  27.3 20.2 %copy-start = (f32[512,256]{1,0:T(8,128)S(1)}, f32[512,256]{1,0:T(8,128)}, u32[]{:S(2)}) copy-start(f32[512,256]{1,0:T(8,128)} %param.15) | copy-start | bytes 1572868
  27.3 20.2 %copy-start.1 = (f32[8,256]{1,0:T(8,128)S(1)}, f32[8,256]{1,0:T(8,128)}, u32[]{:S(2)}) copy-start(f32[8,256]{1,0:T(8,128)} %param.14) | copy-start | bytes 24580
  47.6 66.7 %reduce-scatter.2.cloned.1.call-start = ((), (), s32[]{:S(2)}) async-start(), calls=%async_computation.4 | async-start | bytes 1179648 | tf_op jit(solution)/shard_map/while/body/eval_jaxpr/reduce_scatter | solution.py:25
  140.0 63.7 %reduce-scatter.2.cloned.1.call-start = ((), (), s32[]{:S(2)}) async-start(), calls=%async_computation.4 | async-start | bytes 1179648 | tf_op jit(solution)/shard_map/while/body/eval_jaxpr/reduce_scatter | solution.py:25
  229.4 63.8 %reduce-scatter.2.cloned.1.call-start = ((), (), s32[]{:S(2)}) async-start(), calls=%async_computation.4 | async-start | bytes 1179648 | tf_op jit(solution)/shard_map/while/body/eval_jaxpr/reduce_scatter | solution.py:25
  318.8 63.8 %reduce-scatter.2.cloned.1.call-start = ((), (), s32[]{:S(2)}) async-start(), calls=%async_computation.4 | async-start | bytes 1179648 | tf_op jit(solution)/shard_map/while/body/eval_jaxpr/reduce_scatter | solution.py:25
  415.4 10.4 %all-to-all-start.1 = ((f32[4,128,256]{2,1,0:T(8,128)}), f32[4,128,256]{2,1,0:T(8,128)S(1)}, u32[]{:S(2)}, u32[]{:S(2)}) async-start(f32[4,128,256]{2,1,0:T(8,128)} %get-tuple-element.318), calls=%async_computation.2 | async-start | bytes 1048576 | tf_op jit(solution)/shard_map/all_to_all | solution.py:68
Sparse Core Ops, SparseCore 0:
  81.4 32.8 reduce-scatter.1
  173.9 29.8 reduce-scatter.1
  263.3 29.8 reduce-scatter.1
  352.6 29.8 reduce-scatter.1
where the time goes:
time: 435 us; the launch traced here: 434 us
  waiting for transfers between devices  130 us (30%)
  blocking collectives  121 us (28%)
  local copies, waits for them, and re-layouts  107 us (25%)
  matrix products  52.2 us (12%)
  between operations  13.8 us (3%)
  starting transfers between devices  8.82 us (2%)
    reduce_scatter x4, waiting for transfers between devices, backup(): lax.psum_scatter(partial_value, 'state', scatter_dimension=1, tiled=True)  123 us
    gather x8, local copies, waits for them, and re-layouts, backup(): picked = next_alphas[next_rows]  88.1 us
    psum x4, blocking collectives, backup(): lax.psum(jnp.sum(belief_rows * section_alphas, axis=1), 'state')  54.7 us
    all_gather x4, blocking collectives, turn(): nextset = lax.all_gather(part_alphas, 'section', axis=0, tiled=True)  40.1 us
    dot_general x4, matrix products, backup(): jnp.dot(masked, trans_flat, preferred_element_type=jnp.float32)  23.1 us
    dot_general x4, matrix products, backup(): jnp.einsum('bos,aos->bas', picked, obs_table, precision=lax.Precision.HIG...  21.9 us
    while x2, local copies, waits for them, and re-layouts, local(): result = lax.fori_loop(0, sections, turn, start)  12.7 us
    all_gather x1, blocking collectives, local(): lax.all_gather(action, 'section', axis=0, tiled=True)  11.2 us
  transfers between devices with their start and end apart: 6, of which 5 were waited for; matrix products, arithmetic and copies ran while one was open for 3% of the time, Pallas kernels for 0%

commit v1 on v0

--- a/solution.py
+++ b/solution.py
@@ -25,7 +25,9 @@
     summed = lax.psum_scatter(partial_value, "state", scatter_dimension=1, tiled=True)
     reward_rows = jnp.dot(onehot, reward, precision=lax.Precision.HIGHEST)
     section_alphas = reward_rows + discount * summed
-    section_values = lax.psum(jnp.sum(belief_rows * section_alphas, axis=1), "state")
+    patch = jnp.sum(belief_rows * section_alphas, axis=1)
+    after = lax.all_gather(patch, "state")
+    section_values = jnp.sum(after, axis=0)
     return (section_alphas, section_values)
 
 

time: 435 us -> 420 us (0.966)
  blocking collectives: 121 us -> 104 us
    psum x4 -> x0, blocking collectives: 54.7 us -> none  [backup(): lax.psum(jnp.sum(belief_rows * section_alphas, axis=1), 'state')]
    all_gather x0 -> x4, blocking collectives: none -> 37.4 us  [backup(): after = lax.all_gather(patch, 'state')]
where the time goes in v1:
time: 420 us; the launch traced here: 419 us
  waiting for transfers between devices  132 us (31%)
  local copies, waits for them, and re-layouts  107 us (25%)
  blocking collectives  104 us (25%)
  matrix products  52.2 us (12%)
  between operations  13.8 us (3%)
  starting transfers between devices  8.82 us (2%)
    reduce_scatter x4, waiting for transfers between devices, backup(): lax.psum_scatter(partial_value, 'state', scatter_dimension=1, tiled=True)  124 us
    gather x8, local copies, waits for them, and re-layouts, backup(): picked = next_alphas[next_rows]  88.1 us
    all_gather x4, blocking collectives, turn(): nextset = lax.all_gather(part_alphas, 'section', axis=0, tiled=True)  40.4 us
    all_gather x4, blocking collectives, backup(): after = lax.all_gather(patch, 'state')  37.4 us
    dot_general x4, matrix products, backup(): jnp.dot(masked, trans_flat, preferred_element_type=jnp.float32)  23.1 us
    dot_general x4, matrix products, backup(): jnp.einsum('bos,aos->bas', picked, obs_table, precision=lax.Precision.HIG...  21.9 us
    while x2, local copies, waits for them, and re-layouts, local(): result = lax.fori_loop(0, sections, turn, start)  12.7 us
    all_gather x1, blocking collectives, local(): lax.all_gather(action, 'section', axis=0, tiled=True)  11.2 us
  transfers between devices with their start and end apart: 6, of which 5 were waited for; matrix products, arithmetic and copies ran while one was open for 3% of the time, Pallas kernels for 0%

profile of v1, /device:TPU:0, one launch (start us, length us, event | category | flops | bytes accessed | tf_op | source)
XLA Modules:
  0.0 418.7 jit_solution(4748796631810239418)
XLA Ops:
  14.7 11.2 %all-gather.2 = s32[4,1,512]{2,1,0:T(1,128)S(1)} all-gather(s32[1,1,512]{2,1,0:T(1,128)} %bitcast.68), channel_id=1, replica_groups=mesh['section'=4,'state'=8] {'section'}, dimensions={0}, use_global_device_ids=true | all-gather | bytes 10240 | tf_op jit(solution)/shard_map/all_gather | solution.py:41
  27.4 11.3 %copy.20 = bf16[8,256,2048]{2,0,1:T(8,128)(2,1)} copy(bf16[8,256,2048]{2,1,0:T(8,128)(2,1)} %param.13) | data formatting | bytes 16777216 | tf_op jit(solution)/shard_map/while | solution.py:68
  38.7 8.0 %all_gather.40 = s32[4,512,32]{1,2,0:T(8,128)S(1)} all-gather(s32[1,512,32]{1,2,0:T(8,128)S(1)} %copy-done.2), channel_id=1, replica_groups=mesh['section'=4,'state'=8] {'section'}, dimensions={0}, use_global_device_ids=true | all-gather | bytes 327680 | tf_op jit(solution)/shard_map/all_gather | solution.py:42
  47.6 345.1 %while.20 = (s32[]{:T(128)}, f32[512,256]{1,0:T(8,128)S(1)}, f32[4,128,256]{2,1,0:T(8,128)}, f32[4,128]{1,0:T(4,128)S(1)}, s32[4,512]{1,0:T(4,128)S(1)}, /*index...) while((s32[]{:T(128)}, f32[512,256]{1,0:T(8,128)S(1)}, ...), condition=%wide.region_4.5_spmd, body=%wide.region_0.4_spmd.sunk | while | flops 1178226432 | bytes 36778776 | solution.py:68
  47.9 16.1 %gather_fusion = f32[4096,256]{1,0:T(8,128)} fusion(f32[512,256]{1,0:T(8,128)S(1)} %get-tuple-element.454, s32[4096]{0:T(1024)S(1)} %broadcast_clamp_fusion.2), kind=kCustom, calls=%fused_computation.clone.1 | custom fusion | bytes 8404992 | tf_op jit(solution)/shard_map/while/body/eval_jaxpr/gather | solution.py:13
  64.0 5.9 %copy.29 = f32[128,32,256]{0,1,2:T(8,128)} copy(f32[128,32,256]{2,1,0:T(8,128)} %bitcast.60) | data formatting | bytes 8388608 | tf_op jit(solution)/shard_map/while/body/eval_jaxpr/gather | solution.py:13
  70.0 5.5 %fusion.24 = bf16[128,8,256]{0,1,2:T(8,128)(2,1)S(1)} fusion(f32[128,32,256]{0,1,2:T(8,128)} %copy.29, f32[8,32,256]{1,0,2:T(8,128)S(1)} %get-tuple-element.477, f32[128,8]{0,1:T(8,128)S(1)} %fusion.23), kind=kOutput, calls=%fused_computation.4.clone.1 | convolution fusion | flops 101187584 | bytes 4984832 | tf_op jit(solution)/shard_map/while/body/eval_jaxpr/bos,aos->bas/dot_general | solution.py:14
  75.5 5.8 %convolution_bitcast_fusion.2 = f32[128,2048]{1,0:T(8,128)} fusion(bf16[128,8,256]{0,1,2:T(8,128)(2,1)S(1)} %fusion.24, bf16[8,256,2048]{2,0,1:T(8,128)(2,1)} %get-tuple-element.478), kind=kOutput, calls=%fused_computation.1.clone.1 | convolution fusion | flops 1073741824 | bytes 9961472 | tf_op jit(solution)/shard_map/while/body/eval_jaxpr/dot_general | solution.py:24
  81.3 33.0 %reduce-scatter.2.cloned.1.call-done = f32[128,256]{1,0:T(8,128)} async-done(((f32[128,2048]{1,0:T(8,128)}), f32[128,256]{1,0:T(8,128)}) %reduce-scatter.2.cloned.1.call-update) | async-done | bytes 131088 | tf_op jit(solution)/shard_map/while/body/eval_jaxpr/reduce_scatter | solution.py:25
  116.1 10.1 %all_gather.42 = f32[512,256]{1,0:T(8,128)S(1)} all-gather(f32[128,256]{1,0:T(8,128)S(1)} %get-tuple-element.435), channel_id=1, replica_groups=mesh['section'=4,'state'=8] {'section'}, dimensions={0}, use_global_device_ids=true | all-gather | bytes 655360 | tf_op jit(solution)/shard_map/while/body/eval_jaxpr/all_gather | solution.py:58
  126.3 9.3 %all-gather.4 = f32[8,1,128]{2,1,0:T(1,128)S(1)} all-gather(f32[1,1,128]{2,1,0:T(1,128)S(1)} %bitcast.63), channel_id=2, replica_groups=mesh['section'=4,'state'=8] {'state'}, dimensions={0}, use_global_device_ids=true | all-gather | bytes 4608 | tf_op jit(solution)/shard_map/while/body/eval_jaxpr/all_gather | solution.py:29
  136.1 16.1 %gather_fusion = f32[4096,256]{1,0:T(8,128)} fusion(f32[512,256]{1,0:T(8,128)S(1)} %get-tuple-element.454, s32[4096]{0:T(1024)S(1)} %broadcast_clamp_fusion.2), kind=kCustom, calls=%fused_computation.clone.1 | custom fusion | bytes 8404992 | tf_op jit(solution)/shard_map/while/body/eval_jaxpr/gather | solution.py:13
  152.2 5.9 %copy.29 = f32[128,32,256]{0,1,2:T(8,128)} copy(f32[128,32,256]{2,1,0:T(8,128)} %bitcast.60) | data formatting | bytes 8388608 | tf_op jit(solution)/shard_map/while/body/eval_jaxpr/gather | solution.py:13
  163.6 5.8 %convolution_bitcast_fusion.2 = f32[128,2048]{1,0:T(8,128)} fusion(bf16[128,8,256]{0,1,2:T(8,128)(2,1)S(1)} %fusion.24, bf16[8,256,2048]{2,0,1:T(8,128)(2,1)} %get-tuple-element.478), kind=kOutput, calls=%fused_computation.1.clone.1 | convolution fusion | flops 1073741824 | bytes 9961472 | tf_op jit(solution)/shard_map/while/body/eval_jaxpr/dot_general | solution.py:24
  169.4 30.5 %reduce-scatter.2.cloned.1.call-done = f32[128,256]{1,0:T(8,128)} async-done(((f32[128,2048]{1,0:T(8,128)}), f32[128,256]{1,0:T(8,128)}) %reduce-scatter.2.cloned.1.call-update) | async-done | bytes 131088 | tf_op jit(solution)/shard_map/while/body/eval_jaxpr/reduce_scatter | solution.py:25
  201.7 10.1 %all_gather.42 = f32[512,256]{1,0:T(8,128)S(1)} all-gather(f32[128,256]{1,0:T(8,128)S(1)} %get-tuple-element.435), channel_id=1, replica_groups=mesh['section'=4,'state'=8] {'section'}, dimensions={0}, use_global_device_ids=true | all-gather | bytes 655360 | tf_op jit(solution)/shard_map/while/body/eval_jaxpr/all_gather | solution.py:58
  211.9 9.4 %all-gather.4 = f32[8,1,128]{2,1,0:T(1,128)S(1)} all-gather(f32[1,1,128]{2,1,0:T(1,128)S(1)} %bitcast.63), channel_id=2, replica_groups=mesh['section'=4,'state'=8] {'state'}, dimensions={0}, use_global_device_ids=true | all-gather | bytes 4608 | tf_op jit(solution)/shard_map/while/body/eval_jaxpr/all_gather | solution.py:29
  221.7 16.1 %gather_fusion = f32[4096,256]{1,0:T(8,128)} fusion(f32[512,256]{1,0:T(8,128)S(1)} %get-tuple-element.454, s32[4096]{0:T(1024)S(1)} %broadcast_clamp_fusion.2), kind=kCustom, calls=%fused_computation.clone.1 | custom fusion | bytes 8404992 | tf_op jit(solution)/shard_map/while/body/eval_jaxpr/gather | solution.py:13
  237.8 5.9 %copy.29 = f32[128,32,256]{0,1,2:T(8,128)} copy(f32[128,32,256]{2,1,0:T(8,128)} %bitcast.60) | data formatting | bytes 8388608 | tf_op jit(solution)/shard_map/while/body/eval_jaxpr/gather | solution.py:13
  243.8 5.5 %fusion.24 = bf16[128,8,256]{0,1,2:T(8,128)(2,1)S(1)} fusion(f32[128,32,256]{0,1,2:T(8,128)} %copy.29, f32[8,32,256]{1,0,2:T(8,128)S(1)} %get-tuple-element.477, f32[128,8]{0,1:T(8,128)S(1)} %fusion.23), kind=kOutput, calls=%fused_computation.4.clone.1 | convolution fusion | flops 101187584 | bytes 4984832 | tf_op jit(solution)/shard_map/while/body/eval_jaxpr/bos,aos->bas/dot_general | solution.py:14
  249.2 5.8 %convolution_bitcast_fusion.2 = f32[128,2048]{1,0:T(8,128)} fusion(bf16[128,8,256]{0,1,2:T(8,128)(2,1)S(1)} %fusion.24, bf16[8,256,2048]{2,0,1:T(8,128)(2,1)} %get-tuple-element.478), kind=kOutput, calls=%fused_computation.1.clone.1 | convolution fusion | flops 1073741824 | bytes 9961472 | tf_op jit(solution)/shard_map/while/body/eval_jaxpr/dot_general | solution.py:24
  255.0 30.5 %reduce-scatter.2.cloned.1.call-done = f32[128,256]{1,0:T(8,128)} async-done(((f32[128,2048]{1,0:T(8,128)}), f32[128,256]{1,0:T(8,128)}) %reduce-scatter.2.cloned.1.call-update) | async-done | bytes 131088 | tf_op jit(solution)/shard_map/while/body/eval_jaxpr/reduce_scatter | solution.py:25
  287.4 10.2 %all_gather.42 = f32[512,256]{1,0:T(8,128)S(1)} all-gather(f32[128,256]{1,0:T(8,128)S(1)} %get-tuple-element.435), channel_id=1, replica_groups=mesh['section'=4,'state'=8] {'section'}, dimensions={0}, use_global_device_ids=true | all-gather | bytes 655360 | tf_op jit(solution)/shard_map/while/body/eval_jaxpr/all_gather | solution.py:58
  297.7 9.5 %all-gather.4 = f32[8,1,128]{2,1,0:T(1,128)S(1)} all-gather(f32[1,1,128]{2,1,0:T(1,128)S(1)} %bitcast.63), channel_id=2, replica_groups=mesh['section'=4,'state'=8] {'state'}, dimensions={0}, use_global_device_ids=true | all-gather | bytes 4608 | tf_op jit(solution)/shard_map/while/body/eval_jaxpr/all_gather | solution.py:29
  307.6 16.1 %gather_fusion = f32[4096,256]{1,0:T(8,128)} fusion(f32[512,256]{1,0:T(8,128)S(1)} %get-tuple-element.454, s32[4096]{0:T(1024)S(1)} %broadcast_clamp_fusion.2), kind=kCustom, calls=%fused_computation.clone.1 | custom fusion | bytes 8404992 | tf_op jit(solution)/shard_map/while/body/eval_jaxpr/gather | solution.py:13
  323.7 5.9 %copy.29 = f32[128,32,256]{0,1,2:T(8,128)} copy(f32[128,32,256]{2,1,0:T(8,128)} %bitcast.60) | data formatting | bytes 8388608 | tf_op jit(solution)/shard_map/while/body/eval_jaxpr/gather | solution.py:13
  335.2 5.8 %convolution_bitcast_fusion.2 = f32[128,2048]{1,0:T(8,128)} fusion(bf16[128,8,256]{0,1,2:T(8,128)(2,1)S(1)} %fusion.24, bf16[8,256,2048]{2,0,1:T(8,128)(2,1)} %get-tuple-element.478), kind=kOutput, calls=%fused_computation.1.clone.1 | convolution fusion | flops 1073741824 | bytes 9961472 | tf_op jit(solution)/shard_map/while/body/eval_jaxpr/dot_general | solution.py:24
  341.0 30.4 %reduce-scatter.2.cloned.1.call-done = f32[128,256]{1,0:T(8,128)} async-done(((f32[128,2048]{1,0:T(8,128)}), f32[128,256]{1,0:T(8,128)}) %reduce-scatter.2.cloned.1.call-update) | async-done | bytes 131088 | tf_op jit(solution)/shard_map/while/body/eval_jaxpr/reduce_scatter | solution.py:25
  373.2 10.0 %all_gather.42 = f32[512,256]{1,0:T(8,128)S(1)} all-gather(f32[128,256]{1,0:T(8,128)S(1)} %get-tuple-element.435), channel_id=1, replica_groups=mesh['section'=4,'state'=8] {'section'}, dimensions={0}, use_global_device_ids=true | all-gather | bytes 655360 | tf_op jit(solution)/shard_map/while/body/eval_jaxpr/all_gather | solution.py:58
  383.3 9.3 %all-gather.4 = f32[8,1,128]{2,1,0:T(1,128)S(1)} all-gather(f32[1,1,128]{2,1,0:T(1,128)S(1)} %bitcast.63), channel_id=2, replica_groups=mesh['section'=4,'state'=8] {'state'}, dimensions={0}, use_global_device_ids=true | all-gather | bytes 4608 | tf_op jit(solution)/shard_map/while/body/eval_jaxpr/all_gather | solution.py:29
  392.6 7.3 %all_to_all.40 = f32[4,1,128]{2,1,0:T(1,128)S(1)} all-to-all(f32[4,1,128]{2,1,0:T(1,128)S(1)} %bitcast.66), channel_id=1, replica_groups=mesh['section'=4,'state'=8] {'section'}, dimensions={0} | all-to-all | bytes 4096 | tf_op jit(solution)/shard_map/all_to_all | solution.py:71
  403.4 7.3 %all-to-all-done.1 = f32[4,128,256]{2,1,0:T(8,128)S(1)} async-done(((f32[4,128,256]{2,1,0:T(8,128)}), f32[4,128,256]{2,1,0:T(8,128)S(1)}, u32[]{:S(2)}, u32[]{:S(2)}) %all-to-all-start.1) | async-done | bytes 524320 | tf_op jit(solution)/shard_map/all_to_all | solution.py:70
  (71 shorter events, 35.2 us)
Async XLA Ops:
  9.5 37.1 %all-to-all-start = ((f32[1,512,256]{2,0,1:T(1,128)}), f32[1,512,256]{2,0,1:T(1,128)S(1)}, u32[]{:S(2)}, u32[]{:S(2)}) async-start(f32[1,512,256]{2,0,1:T(1,128)} %copy.17), calls=%async_computation.1 | async-start | bytes 1048576 | tf_op jit(solution)/shard_map/all_to_all | solution.py:44
  27.3 11.3 %copy-start.2 = (s32[1,512,32]{1,2,0:T(8,128)S(1)}, s32[1,512,32]{1,2,0:T(8,128)}, u32[]{:S(2)}) copy-start(s32[1,512,32]{1,2,0:T(8,128)} %param.11) | copy-start | bytes 196612
  27.3 20.2 %copy-start = (f32[512,256]{1,0:T(8,128)S(1)}, f32[512,256]{1,0:T(8,128)}, u32[]{:S(2)}) copy-start(f32[512,256]{1,0:T(8,128)} %param.15) | copy-start | bytes 1572868
  27.3 20.2 %copy-start.1 = (f32[8,256]{1,0:T(8,128)S(1)}, f32[8,256]{1,0:T(8,128)}, u32[]{:S(2)}) copy-start(f32[8,256]{1,0:T(8,128)} %param.14) | copy-start | bytes 24580
  47.6 66.7 %reduce-scatter.2.cloned.1.call-start = ((), (), s32[]{:S(2)}) async-start(), calls=%async_computation.4 | async-start | bytes 1179648 | tf_op jit(solution)/shard_map/while/body/eval_jaxpr/reduce_scatter | solution.py:25
  135.7 64.2 %reduce-scatter.2.cloned.1.call-start = ((), (), s32[]{:S(2)}) async-start(), calls=%async_computation.4 | async-start | bytes 1179648 | tf_op jit(solution)/shard_map/while/body/eval_jaxpr/reduce_scatter | solution.py:25
  221.3 64.2 %reduce-scatter.2.cloned.1.call-start = ((), (), s32[]{:S(2)}) async-start(), calls=%async_computation.4 | async-start | bytes 1179648 | tf_op jit(solution)/shard_map/while/body/eval_jaxpr/reduce_scatter | solution.py:25
  307.2 64.1 %reduce-scatter.2.cloned.1.call-start = ((), (), s32[]{:S(2)}) async-start(), calls=%async_computation.4 | async-start | bytes 1179648 | tf_op jit(solution)/shard_map/while/body/eval_jaxpr/reduce_scatter | solution.py:25
  400.0 10.8 %all-to-all-start.1 = ((f32[4,128,256]{2,1,0:T(8,128)}), f32[4,128,256]{2,1,0:T(8,128)S(1)}, u32[]{:S(2)}, u32[]{:S(2)}) async-start(f32[4,128,256]{2,1,0:T(8,128)} %get-tuple-element.318), calls=%async_computation.2 | async-start | bytes 1048576 | tf_op jit(solution)/shard_map/all_to_all | solution.py:70
Sparse Core Ops, SparseCore 0:
  81.4 32.8 reduce-scatter.1
  169.5 30.3 reduce-scatter.1
  255.2 30.3 reduce-scatter.1
  341.1 30.2 reduce-scatter.1
